TPU v7x, 32 devices: a whole 2x2x4 slice. The times are simulated.
32 devices in a mesh: grp: 2 (over y), slab: 2 (over x), lat: 8 (over z, core).
Axes of the slice: x: 2, y: 2, z: 4, core: 2. Of those that a mesh axis runs over, the one named last changes fastest.
Arguments:
- cond_lists: int32 [64, 16], P(('slab', 'lat')), may hold values from 0 to 31, all different within a row
- regress: float32 [64, 128, 2048], P(('slab', 'lat')), may hold values from -0.09375 to 0.09375
- chol: float32 [64, 128, 128], P(('slab', 'lat')), as said below
- noise: float32 [128, 256, 128], P(('grp', 'slab', 'lat')), parts along dimension 0, may hold values from -6 to 6
- start_field: float32 [64, 256, 128], P(('grp', 'lat')), parts along dimension 0, may hold values from -6 to 6
Outputs:
- field: float32 [128, 256, 128], P(('grp', 'slab', 'lat')), parts along dimension 0
There are 2 independent parts, one for each index of `grp`. A program takes and returns all parts, laid end to end along the dimension named above; an argument that names none is the same for every part. Nothing has to cross between parts.
Inputs may be any that keep to these rules, and one draw needn't show every extreme that they name: `cond_lists`: each row names 16 distinct positions of the previous slab. `chol`: each factor is lower triangular with diagonal entries from 0.3 to 0.7.
All inputs are finite; a program needn't handle non-finite values.
Results may differ from a plain program's by a relative error of at most 0.0001.
Values sent between devices are 32-bit elements; how exact they have to be, the bound alone decides.
No kernel may reach another device: no remote copies, remote signals or barrier semaphores. Data moves between devices by JAX's collectives and lax.ppermute only.
A program may use at most 64 MiB of HBM per device.

v0:
```python
import jax
import jax.numpy as jnp
from jax import lax
from jax.sharding import PartitionSpec as P

PANEL = 64


def passed_along(array, axis, by):
    length = lax.axis_size(axis)
    pairs = [(i, i + by) for i in range(length) if 0 <= i + by < length]
    return lax.ppermute(array, axis, pairs)


def shards(cond_lists, regress, chol, noise, start_field):
    blocks, nreal_here, block_size = noise.shape
    list_length = cond_lists.shape[1]
    front_width = PANEL
    fronts = nreal_here // front_width
    n_slab = lax.axis_size("slab")
    slab_pos = lax.axis_index("slab")
    sections = n_slab + fronts - 1
    factors = regress.reshape(blocks, block_size, list_length, block_size)

    def compute(front_start, previous):
        picked = previous[cond_lists]
        shocks = lax.dynamic_slice_in_dim(noise, front_start, front_width, 1)
        mean_part = jnp.einsum("jakb,jkwb->jwa", factors, picked, precision=lax.Precision.HIGHEST)
        shock_part = jnp.einsum("jab,jwb->jwa", chol, shocks, precision=lax.Precision.HIGHEST)
        return mean_part + shock_part

    def skip(front_start, previous):
        return jnp.zeros((blocks, front_width, block_size), jnp.float32)

    start_box = jnp.zeros((blocks, front_width, block_size), jnp.float32)

    def section(section_step, carry):
        incoming, field_out = carry
        front_index = section_step - slab_pos
        active = (front_index >= 0) & (front_index < fronts)
        front_start = jnp.clip(front_index, 0, fronts - 1) * front_width
        boundary = lax.dynamic_slice_in_dim(start_field, front_start, front_width, 1)
        source = jnp.where(slab_pos == 0, boundary, incoming)
        previous = lax.all_gather(source, "lat", axis=0, tiled=True)
        fresh_blocks = lax.cond(active, compute, skip, front_start, previous)
        old_blocks = lax.dynamic_slice_in_dim(field_out, front_start, front_width, 1)
        kept = jnp.where(active, fresh_blocks, old_blocks)
        field_out = lax.dynamic_update_slice_in_dim(field_out, kept, front_start, 1)
        incoming = passed_along(fresh_blocks, "slab", 1)
        return (incoming, field_out)

    start_out = jnp.zeros((blocks, nreal_here, block_size), jnp.float32)
    incoming, field_out = lax.fori_loop(0, sections, section, (start_box, start_out))
    return field_out


def solution(mesh):
    in_specs = (
        P(("slab", "lat"), None),
        P(("slab", "lat"), None, None),
        P(("slab", "lat"), None, None),
        P(("grp", "slab", "lat"), None, None),
        P(("grp", "lat"), None, None),
    )
    out_specs = P(("grp", "slab", "lat"), None, None)
    return jax.shard_map(shards, mesh=mesh, in_specs=in_specs, out_specs=out_specs, check_vma=False)
```

profile of v0, /device:TPU:0, one launch (start us, length us, event | category | flops | bytes accessed | tf_op | source)
XLA Modules:
  0.0 231.9 jit_solution(2512306260924469446)
XLA Ops:
  6.5 5.4 %copy.8 = f32[4,128,2048]{1,2,0:T(8,128)} copy(f32[4,128,2048]{2,1,0:T(8,128)} %param.10) | data formatting | bytes 8388608 | tf_op args[1]
  11.9 5.4 %copy.9 = f32[4,128,16,128]{3,1,2,0:T(8,128)} copy(f32[4,128,16,128]{1,3,2,0:T(8,128)} %bitcast.9) | data formatting | bytes 8388608 | tf_op jit(solution)/shard_map/while | solution.py:53
  17.4 207.3 %while.16 = (s32[]{:T(128)}, f32[4,64,128]{2,1,0:T(8,128)S(1)}, f32[4,256,128]{2,1,0:T(8,128)S(1)}, s32[]{:T(128)}, pred[]{:T(512)}, /*index=5*/f32[4,256,128]{2...) while((s32[]{:T(128)}, f32[4,64,128]{2,1,0:T(8,128)S(1)}, ...), condition=%wide.region_3.4_spmd, body=%wide.region_0.3_spmd.sunk | while | flops 855737536 | bytes 16127929 | solution.py:53
  17.4 1.6 dynamic-slice_select_fusion.2
  19.1 25.7 %all-gather.2.cloned.1.call-done = f32[32,64,128]{2,1,0:T(8,128)} async-done(((f32[4,64,128]{2,1,0:T(8,128)}), f32[32,64,128]{2,1,0:T(8,128)}) %all-gather.2.cloned.1.call-update) | async-done | bytes 1048592 | tf_op jit(solution)/shard_map/while/body/eval_jaxpr/all_gather | solution.py:44
  44.8 9.7 %conditional.2 = (f32[4,64,128]{2,1,0:T(8,128)S(1)}) conditional(s32[]{:T(128)} %convert_element_type.9, () %tuple.42, (s32[4,16]{1,0:T(4,128)S(1)}, f32[32,64,128]{2,1,0:T(8,128)}, f32[4,128,16,128]{3,1,2,0:T(8,128)}, s32[]{:T(128)}, f32[4,256,128]{2,1,0:T(8,128)}, /*index=5*/f32[4,128,128]{2,1,0:T(8,128)S(1)}) %tuple.43), branch_computations={%region_1.1_spmd, %region_2.2_spmd} | conditional | flops 855672000 | bytes 11277870 | solution.py:45
  44.9 1.9 gather_fusion
  46.8 6.2 %convolution_bitcast_fusion = f32[4,64,128]{2,1,0:T(8,128)S(1)} fusion(f32[4,16,64,128]{3,2,1,0:T(8,128)S(1)} %bitcast.8, f32[4,128,16,128]{3,1,2,0:T(8,128)} %get-tuple-element.210), kind=kOutput, calls=%fused_computation.2 | convolution fusion | flops 805306368 | bytes 6422528 | tf_op jit(solution)/shard_map/while/body/eval_jaxpr/cond/branch_1_fun/jakb,jkwb->jwa/dot_general | solution.py:28
  55.8 3.4 %collective-permute-done = f32[4,64,128]{2,1,0:T(8,128)S(1)} collective-permute-done((f32[4,64,128]{2,1,0:T(8,128)S(1)}, f32[4,64,128]{2,1,0:T(8,128)S(1)}, u32[]{:S(2)}, u32[]{:S(2)}) %collective-permute-start) | collective-permute-done | bytes 131104 | tf_op jit(solution)/shard_map/while/body/eval_jaxpr/ppermute | solution.py:12
  60.8 23.6 %all-gather.2.cloned.1.call-done = f32[32,64,128]{2,1,0:T(8,128)} async-done(((f32[4,64,128]{2,1,0:T(8,128)}), f32[32,64,128]{2,1,0:T(8,128)}) %all-gather.2.cloned.1.call-update) | async-done | bytes 1048592 | tf_op jit(solution)/shard_map/while/body/eval_jaxpr/all_gather | solution.py:44
  84.4 9.7 %conditional.2 = (f32[4,64,128]{2,1,0:T(8,128)S(1)}) conditional(s32[]{:T(128)} %convert_element_type.9, () %tuple.42, (s32[4,16]{1,0:T(4,128)S(1)}, f32[32,64,128]{2,1,0:T(8,128)}, f32[4,128,16,128]{3,1,2,0:T(8,128)}, s32[]{:T(128)}, f32[4,256,128]{2,1,0:T(8,128)}, /*index=5*/f32[4,128,128]{2,1,0:T(8,128)S(1)}) %tuple.43), branch_computations={%region_1.1_spmd, %region_2.2_spmd} | conditional | flops 855672000 | bytes 11277870 | solution.py:45
  84.5 1.9 gather_fusion
  86.4 6.2 %convolution_bitcast_fusion = f32[4,64,128]{2,1,0:T(8,128)S(1)} fusion(f32[4,16,64,128]{3,2,1,0:T(8,128)S(1)} %bitcast.8, f32[4,128,16,128]{3,1,2,0:T(8,128)} %get-tuple-element.210), kind=kOutput, calls=%fused_computation.2 | convolution fusion | flops 805306368 | bytes 6422528 | tf_op jit(solution)/shard_map/while/body/eval_jaxpr/cond/branch_1_fun/jakb,jkwb->jwa/dot_general | solution.py:28
  94.2 3.4 %collective-permute-start = (f32[4,64,128]{2,1,0:T(8,128)S(1)}, f32[4,64,128]{2,1,0:T(8,128)S(1)}, u32[]{:S(2)}, u32[]{:S(2)}) collective-permute-start(f32[4,64,128]{2,1,0:T(8,128)S(1)} %get-tuple-element.376), channel_id=1, source_target_pairs={{0,8},{1,9},{2,10},{3,11},{4,12},{5,13},{6,14},{7,15},{16,24},{17,... | collective-permute-start | bytes 393224 | tf_op jit(solution)/shard_map/while/body/eval_jaxpr/ppermute | solution.py:12
  97.6 3.1 %collective-permute-done = f32[4,64,128]{2,1,0:T(8,128)S(1)} collective-permute-done((f32[4,64,128]{2,1,0:T(8,128)S(1)}, f32[4,64,128]{2,1,0:T(8,128)S(1)}, u32[]{:S(2)}, u32[]{:S(2)}) %collective-permute-start) | collective-permute-done | bytes 131104 | tf_op jit(solution)/shard_map/while/body/eval_jaxpr/ppermute | solution.py:12
  100.7 1.6 dynamic-slice_select_fusion.2
  102.3 23.7 %all-gather.2.cloned.1.call-done = f32[32,64,128]{2,1,0:T(8,128)} async-done(((f32[4,64,128]{2,1,0:T(8,128)}), f32[32,64,128]{2,1,0:T(8,128)}) %all-gather.2.cloned.1.call-update) | async-done | bytes 1048592 | tf_op jit(solution)/shard_map/while/body/eval_jaxpr/all_gather | solution.py:44
  126.0 9.7 %conditional.2 = (f32[4,64,128]{2,1,0:T(8,128)S(1)}) conditional(s32[]{:T(128)} %convert_element_type.9, () %tuple.42, (s32[4,16]{1,0:T(4,128)S(1)}, f32[32,64,128]{2,1,0:T(8,128)}, f32[4,128,16,128]{3,1,2,0:T(8,128)}, s32[]{:T(128)}, f32[4,256,128]{2,1,0:T(8,128)}, /*index=5*/f32[4,128,128]{2,1,0:T(8,128)S(1)}) %tuple.43), branch_computations={%region_1.1_spmd, %region_2.2_spmd} | conditional | flops 855672000 | bytes 11277870 | solution.py:45
  126.1 1.9 gather_fusion
  128.0 6.2 %convolution_bitcast_fusion = f32[4,64,128]{2,1,0:T(8,128)S(1)} fusion(f32[4,16,64,128]{3,2,1,0:T(8,128)S(1)} %bitcast.8, f32[4,128,16,128]{3,1,2,0:T(8,128)} %get-tuple-element.210), kind=kOutput, calls=%fused_computation.2 | convolution fusion | flops 805306368 | bytes 6422528 | tf_op jit(solution)/shard_map/while/body/eval_jaxpr/cond/branch_1_fun/jakb,jkwb->jwa/dot_general | solution.py:28
  135.7 3.4 %collective-permute-start = (f32[4,64,128]{2,1,0:T(8,128)S(1)}, f32[4,64,128]{2,1,0:T(8,128)S(1)}, u32[]{:S(2)}, u32[]{:S(2)}) collective-permute-start(f32[4,64,128]{2,1,0:T(8,128)S(1)} %get-tuple-element.376), channel_id=1, source_target_pairs={{0,8},{1,9},{2,10},{3,11},{4,12},{5,13},{6,14},{7,15},{16,24},{17,... | collective-permute-start | bytes 393224 | tf_op jit(solution)/shard_map/while/body/eval_jaxpr/ppermute | solution.py:12
  139.1 3.1 %collective-permute-done = f32[4,64,128]{2,1,0:T(8,128)S(1)} collective-permute-done((f32[4,64,128]{2,1,0:T(8,128)S(1)}, f32[4,64,128]{2,1,0:T(8,128)S(1)}, u32[]{:S(2)}, u32[]{:S(2)}) %collective-permute-start) | collective-permute-done | bytes 131104 | tf_op jit(solution)/shard_map/while/body/eval_jaxpr/ppermute | solution.py:12
  142.2 1.6 dynamic-slice_select_fusion.2
  143.8 23.4 %all-gather.2.cloned.1.call-done = f32[32,64,128]{2,1,0:T(8,128)} async-done(((f32[4,64,128]{2,1,0:T(8,128)}), f32[32,64,128]{2,1,0:T(8,128)}) %all-gather.2.cloned.1.call-update) | async-done | bytes 1048592 | tf_op jit(solution)/shard_map/while/body/eval_jaxpr/all_gather | solution.py:44
  167.2 9.7 %conditional.2 = (f32[4,64,128]{2,1,0:T(8,128)S(1)}) conditional(s32[]{:T(128)} %convert_element_type.9, () %tuple.42, (s32[4,16]{1,0:T(4,128)S(1)}, f32[32,64,128]{2,1,0:T(8,128)}, f32[4,128,16,128]{3,1,2,0:T(8,128)}, s32[]{:T(128)}, f32[4,256,128]{2,1,0:T(8,128)}, /*index=5*/f32[4,128,128]{2,1,0:T(8,128)S(1)}) %tuple.43), branch_computations={%region_1.1_spmd, %region_2.2_spmd} | conditional | flops 855672000 | bytes 11277870 | solution.py:45
  167.3 1.9 gather_fusion
  169.2 6.2 %convolution_bitcast_fusion = f32[4,64,128]{2,1,0:T(8,128)S(1)} fusion(f32[4,16,64,128]{3,2,1,0:T(8,128)S(1)} %bitcast.8, f32[4,128,16,128]{3,1,2,0:T(8,128)} %get-tuple-element.210), kind=kOutput, calls=%fused_computation.2 | convolution fusion | flops 805306368 | bytes 6422528 | tf_op jit(solution)/shard_map/while/body/eval_jaxpr/cond/branch_1_fun/jakb,jkwb->jwa/dot_general | solution.py:28
  176.9 3.4 %collective-permute-start = (f32[4,64,128]{2,1,0:T(8,128)S(1)}, f32[4,64,128]{2,1,0:T(8,128)S(1)}, u32[]{:S(2)}, u32[]{:S(2)}) collective-permute-start(f32[4,64,128]{2,1,0:T(8,128)S(1)} %get-tuple-element.376), channel_id=1, source_target_pairs={{0,8},{1,9},{2,10},{3,11},{4,12},{5,13},{6,14},{7,15},{16,24},{17,... | collective-permute-start | bytes 393224 | tf_op jit(solution)/shard_map/while/body/eval_jaxpr/ppermute | solution.py:12
  180.3 3.1 %collective-permute-done = f32[4,64,128]{2,1,0:T(8,128)S(1)} collective-permute-done((f32[4,64,128]{2,1,0:T(8,128)S(1)}, f32[4,64,128]{2,1,0:T(8,128)S(1)}, u32[]{:S(2)}, u32[]{:S(2)}) %collective-permute-start) | collective-permute-done | bytes 131104 | tf_op jit(solution)/shard_map/while/body/eval_jaxpr/ppermute | solution.py:12
  185.0 23.4 %all-gather.2.cloned.1.call-done = f32[32,64,128]{2,1,0:T(8,128)} async-done(((f32[4,64,128]{2,1,0:T(8,128)}), f32[32,64,128]{2,1,0:T(8,128)}) %all-gather.2.cloned.1.call-update) | async-done | bytes 1048592 | tf_op jit(solution)/shard_map/while/body/eval_jaxpr/all_gather | solution.py:44
  208.4 13.1 %collective-permute-start = (f32[4,64,128]{2,1,0:T(8,128)S(1)}, f32[4,64,128]{2,1,0:T(8,128)S(1)}, u32[]{:S(2)}, u32[]{:S(2)}) collective-permute-start(f32[4,64,128]{2,1,0:T(8,128)S(1)} %get-tuple-element.376), channel_id=1, source_target_pairs={{0,8},{1,9},{2,10},{3,11},{4,12},{5,13},{6,14},{7,15},{16,24},{17,... | collective-permute-start | bytes 393224 | tf_op jit(solution)/shard_map/while/body/eval_jaxpr/ppermute | solution.py:12
  221.5 3.1 %collective-permute-done = f32[4,64,128]{2,1,0:T(8,128)S(1)} collective-permute-done((f32[4,64,128]{2,1,0:T(8,128)S(1)}, f32[4,64,128]{2,1,0:T(8,128)S(1)}, u32[]{:S(2)}, u32[]{:S(2)}) %collective-permute-start) | collective-permute-done | bytes 131104 | tf_op jit(solution)/shard_map/while/body/eval_jaxpr/ppermute | solution.py:12
  (44 shorter events, 12.1 us)
Async XLA Ops:
  11.9 5.4 %copy-start = (f32[4,128,128]{2,1,0:T(8,128)S(1)}, f32[4,128,128]{2,1,0:T(8,128)}, u32[]{:S(2)}) copy-start(f32[4,128,128]{2,1,0:T(8,128)} %param.11) | copy-start | bytes 786436
  11.9 5.5 %copy-start.2 = (s32[4,16]{1,0:T(4,128)S(1)}, s32[4,16]{1,0:T(4,128)}, u32[]{:S(2)}) copy-start(s32[4,16]{1,0:T(4,128)} %param.9) | copy-start | bytes 772
  17.4 27.4 %all-gather.2.cloned.1.call-start = ((), (), s32[]{:S(2)}) async-start(), calls=%async_computation | async-start | bytes 1179648 | tf_op jit(solution)/shard_map/while/body/eval_jaxpr/all_gather | solution.py:44
  54.5 4.7 %collective-permute-start = (f32[4,64,128]{2,1,0:T(8,128)S(1)}, f32[4,64,128]{2,1,0:T(8,128)S(1)}, u32[]{:S(2)}, u32[]{:S(2)}) collective-permute-start(f32[4,64,128]{2,1,0:T(8,128)S(1)} %get-tuple-element.376), channel_id=1, source_target_pairs={{0,8},{1,9},{2,10},{3,11},{4,12},{5,13},{6,14},{7,15},{16,24},{17,... | collective-permute-start | bytes 393224 | tf_op jit(solution)/shard_map/while/body/eval_jaxpr/ppermute | solution.py:12
  59.2 25.2 %all-gather.2.cloned.1.call-start = ((), (), s32[]{:S(2)}) async-start(), calls=%async_computation | async-start | bytes 1179648 | tf_op jit(solution)/shard_map/while/body/eval_jaxpr/all_gather | solution.py:44
  94.2 6.5 %collective-permute-start = (f32[4,64,128]{2,1,0:T(8,128)S(1)}, f32[4,64,128]{2,1,0:T(8,128)S(1)}, u32[]{:S(2)}, u32[]{:S(2)}) collective-permute-start(f32[4,64,128]{2,1,0:T(8,128)S(1)} %get-tuple-element.376), channel_id=1, source_target_pairs={{0,8},{1,9},{2,10},{3,11},{4,12},{5,13},{6,14},{7,15},{16,24},{17,... | collective-permute-start | bytes 393224 | tf_op jit(solution)/shard_map/while/body/eval_jaxpr/ppermute | solution.py:12
  100.7 25.3 %all-gather.2.cloned.1.call-start = ((), (), s32[]{:S(2)}) async-start(), calls=%async_computation | async-start | bytes 1179648 | tf_op jit(solution)/shard_map/while/body/eval_jaxpr/all_gather | solution.py:44
  135.7 6.5 %collective-permute-start = (f32[4,64,128]{2,1,0:T(8,128)S(1)}, f32[4,64,128]{2,1,0:T(8,128)S(1)}, u32[]{:S(2)}, u32[]{:S(2)}) collective-permute-start(f32[4,64,128]{2,1,0:T(8,128)S(1)} %get-tuple-element.376), channel_id=1, source_target_pairs={{0,8},{1,9},{2,10},{3,11},{4,12},{5,13},{6,14},{7,15},{16,24},{17,... | collective-permute-start | bytes 393224 | tf_op jit(solution)/shard_map/while/body/eval_jaxpr/ppermute | solution.py:12
  142.2 25.0 %all-gather.2.cloned.1.call-start = ((), (), s32[]{:S(2)}) async-start(), calls=%async_computation | async-start | bytes 1179648 | tf_op jit(solution)/shard_map/while/body/eval_jaxpr/all_gather | solution.py:44
  176.9 6.5 %collective-permute-start = (f32[4,64,128]{2,1,0:T(8,128)S(1)}, f32[4,64,128]{2,1,0:T(8,128)S(1)}, u32[]{:S(2)}, u32[]{:S(2)}) collective-permute-start(f32[4,64,128]{2,1,0:T(8,128)S(1)} %get-tuple-element.376), channel_id=1, source_target_pairs={{0,8},{1,9},{2,10},{3,11},{4,12},{5,13},{6,14},{7,15},{16,24},{17,... | collective-permute-start | bytes 393224 | tf_op jit(solution)/shard_map/while/body/eval_jaxpr/ppermute | solution.py:12
  183.4 25.0 %all-gather.2.cloned.1.call-start = ((), (), s32[]{:S(2)}) async-start(), calls=%async_computation | async-start | bytes 1179648 | tf_op jit(solution)/shard_map/while/body/eval_jaxpr/all_gather | solution.py:44
  208.4 16.2 %collective-permute-start = (f32[4,64,128]{2,1,0:T(8,128)S(1)}, f32[4,64,128]{2,1,0:T(8,128)S(1)}, u32[]{:S(2)}, u32[]{:S(2)}) collective-permute-start(f32[4,64,128]{2,1,0:T(8,128)S(1)} %get-tuple-element.376), channel_id=1, source_target_pairs={{0,8},{1,9},{2,10},{3,11},{4,12},{5,13},{6,14},{7,15},{16,24},{17,... | collective-permute-start | bytes 393224 | tf_op jit(solution)/shard_map/while/body/eval_jaxpr/ppermute | solution.py:12
  224.6 0.8 copy-start.1
Sparse Core Ops, SparseCore 0:
  19.8 24.9 all-gather.1
  61.6 22.7 all-gather.1
  103.1 22.8 all-gather.1
  144.3 22.8 all-gather.1
  185.5 22.8 all-gather.1
where the time goes:
time: 233 us; the launch traced here: 232 us
  waiting for transfers between devices  136 us (58%)
  matrix products  30.8 us (13%)
  starting transfers between devices  24.6 us (11%)
  local copies, waits for them, and re-layouts  19.6 us (8%)
  between operations  13.1 us (6%)
  other arithmetic  8.07 us (3%)
    all_gather x5, waiting for transfers between devices, section(): previous = lax.all_gather(source, 'lat', axis=0, tiled=True)  120 us
    dot_general x4, matrix products, compute(): jnp.einsum('jakb,jkwb->jwa', factors, picked, precision=lax.Precision.HIG...  24.7 us
    ppermute x5, starting transfers between devices, passed_along(): return lax.ppermute(array, axis, pairs)  24.5 us
    ppermute x5, waiting for transfers between devices, passed_along(): return lax.ppermute(array, axis, pairs)  15.7 us
    select_n x5, other arithmetic, section(): source = jnp.where(slab_pos == 0, boundary, incoming)  7.89 us
    gather x4, local copies, waits for them, and re-layouts, compute(): picked = previous[cond_lists]  7.62 us
    unnamed x7, local copies, waits for them, and re-layouts  6.15 us
    dot_general x4, matrix products, compute(): jnp.einsum('jab,jwb->jwa', chol, shocks, precision=lax.Precision.HIGHEST)  6.13 us
  transfers between devices with their start and end apart: 10, of which 10 were waited for; matrix products, arithmetic and copies ran while one was open for 0% of the time, Pallas kernels for 0%

commit v1 on v0

--- a/solution.py
+++ b/solution.py
@@ -41,7 +41,25 @@
         front_start = jnp.clip(front_index, 0, fronts - 1) * front_width
         boundary = lax.dynamic_slice_in_dim(start_field, front_start, front_width, 1)
         source = jnp.where(slab_pos == 0, boundary, incoming)
-        previous = lax.all_gather(source, "lat", axis=0, tiled=True)
+        ways, here, lap = (lax.axis_size("lat"), lax.axis_index("lat"), source.shape[0])
+        dims = [n * ways if d == 0 else n for d, n in enumerate(source.shape)]
+        full = lax.dynamic_update_slice_in_dim(
+            jnp.zeros(dims, source.dtype), source, here * lap, axis=0
+        )
+        going_up = going_down = source
+        for far in range(1, ways // 2 + 1):
+            going_up = lax.ppermute(going_up, "lat", [(d, (d + 1) % ways) for d in range(ways)])
+            full = lax.dynamic_update_slice_in_dim(
+                full, going_up, (here - far) % ways * lap, axis=0
+            )
+            if 2 * far < ways:
+                going_down = lax.ppermute(
+                    going_down, "lat", [(d, (d - 1) % ways) for d in range(ways)]
+                )
+                full = lax.dynamic_update_slice_in_dim(
+                    full, going_down, (here + far) % ways * lap, axis=0
+                )
+        previous = full
         fresh_blocks = lax.cond(active, compute, skip, front_start, previous)
         old_blocks = lax.dynamic_slice_in_dim(field_out, front_start, front_width, 1)
         kept = jnp.where(active, fresh_blocks, old_blocks)

time: 233 us -> 220 us (0.944)
  waiting for transfers between devices: 136 us -> 76.8 us
  starting transfers between devices: 24.6 us -> 82.3 us
  between operations: 13.1 us -> 0.02 us
  other arithmetic: 8.07 us -> 12.6 us
  local copies, waits for them, and re-layouts: 19.6 us -> 15.6 us
    all_gather x5 -> x0, waiting for transfers between devices: 120 us -> none  [section(): previous = lax.all_gather(source, 'lat', axis=0, tiled=True)]
    ppermute x0 -> x35, waiting for transfers between devices: none -> 72.2 us  [the longest x20 72.1 us: section(): lax.ppermute(going_up, 'lat', [(d, (d + 1) % ways) for d in range(ways)])]
    ppermute x0 -> x35, starting transfers between devices: none -> 54.7 us  [the longest x15 53.9 us: section(): lax.ppermute(going_down, 'lat', [(d, (d - 1) % ways) for d in range(ways)])]
    ppermute x5, waiting for transfers between devices: 15.7 us -> 4.55 us  [passed_along(): return lax.ppermute(array, axis, pairs)]
    dynamic_update_slice x5, other arithmetic: 0.14 us -> 7.93 us  [section(): field_out = lax.dynamic_update_slice_in_dim(field_out, kept, front_start, 1)]
    gather x4, local copies, waits for them, and re-layouts: 7.62 us -> 2.74 us  [compute(): picked = previous[cond_lists]]
    select_n x5, other arithmetic: 7.89 us -> 4.62 us  [section(): source = jnp.where(slab_pos == 0, boundary, incoming)]
    ppermute x5, starting transfers between devices: 24.5 us -> 27.7 us  [passed_along(): return lax.ppermute(array, axis, pairs)]
  transfers between devices with their start and end apart: 10 -> 40, of which waited for: 10 -> 26; matrix products, arithmetic and copies ran while one was open for 0% -> 4% of each run, Pallas kernels for 0% -> 0%
where the time goes in v1:
time: 220 us; the launch traced here: 219 us
  starting transfers between devices  82.3 us (37%)
  waiting for transfers between devices  76.8 us (35%)
  matrix products  30.8 us (14%)
  local copies, waits for them, and re-layouts  15.6 us (7%)
  other arithmetic  12.6 us (6%)
    ppermute x20, waiting for transfers between devices, section(): lax.ppermute(going_up, 'lat', [(d, (d + 1) % ways) for d in range(ways)])  72.1 us
    ppermute x15, starting transfers between devices, section(): lax.ppermute(going_down, 'lat', [(d, (d - 1) % ways) for d in range(ways)])  53.9 us
    ppermute x5, starting transfers between devices, passed_along(): return lax.ppermute(array, axis, pairs)  27.7 us
    dot_general x4, matrix products, compute(): jnp.einsum('jakb,jkwb->jwa', factors, picked, precision=lax.Precision.HIG...  24.7 us
    dynamic_update_slice x5, other arithmetic, section(): field_out = lax.dynamic_update_slice_in_dim(field_out, kept, front_start, 1)  7.93 us
    dot_general x4, matrix products, compute(): jnp.einsum('jab,jwb->jwa', chol, shocks, precision=lax.Precision.HIGHEST)  6.12 us
    while x1, local copies, waits for them, and re-layouts, shards(): lax.fori_loop(0, sections, section, (start_box, start_out))  5.42 us
    unnamed x5, local copies, waits for them, and re-layouts  5.38 us
  transfers between devices with their start and end apart: 40, of which 26 were waited for; matrix products, arithmetic and copies ran while one was open for 4% of the time, Pallas kernels for 0%

profile of v1, /device:TPU:0, one launch (start us, length us, event | category | flops | bytes accessed | tf_op | source)
XLA Modules:
  0.0 219.2 jit_solution(1182586097820858156)
XLA Ops:
  0.0 5.4 %copy.6 = f32[4,128,2048]{1,2,0:T(8,128)} copy(f32[4,128,2048]{2,1,0:T(8,128)} %param.10) | data formatting | bytes 8388608 | tf_op args[1]
  5.4 5.4 %copy.7 = f32[4,128,16,128]{3,1,2,0:T(8,128)} copy(f32[4,128,16,128]{1,3,2,0:T(8,128)} %bitcast.11) | data formatting | bytes 8388608 | tf_op jit(solution)/shard_map/while | solution.py:71
  11.7 207.6 %while.17 = (s32[]{:T(128)}, f32[4,64,128]{2,1,0:T(8,128)S(1)}, f32[4,256,128]{2,1,0:T(8,128)}, s32[]{:T(128)}, pred[]{:T(512)}, /*index=5*/f32[4,256,128]{2,1,0...) while((s32[]{:T(128)}, f32[4,64,128]{2,1,0:T(8,128)S(1)}, ...), condition=%wide.region_3.4_spmd, body=%wide.region_0.3_spmd.sunk | while | flops 855737664 | bytes 19406392 | solution.py:71
  13.2 4.1 %collective-permute-start.1 = (f32[4,64,128]{2,1,0:T(8,128)S(1)}, f32[4,64,128]{2,1,0:T(8,128)S(1)}, u32[]{:S(2)}, u32[]{:S(2)}) collective-permute-start(f32[4,64,128]{2,1,0:T(8,128)S(1)} %dynamic-slice_select_fusion.2), channel_id=1, source_target_pairs={{0,7},{1,0},{2,1},{3,2},{4,3},{5,4},{6,5},{7,6},{8,15},{9,8},{10,9... | collective-permute-start | bytes 393224 | tf_op jit(solution)/shard_map/while/body/eval_jaxpr/ppermute | solution.py:56
  19.9 3.5 %collective-permute-start.3 = (f32[4,64,128]{2,1,0:T(8,128)S(1)}, f32[4,64,128]{2,1,0:T(8,128)S(1)}, u32[]{:S(2)}, u32[]{:S(2)}) collective-permute-start(f32[4,64,128]{2,1,0:T(8,128)S(1)} %collective-permute-done.1), channel_id=1, source_target_pairs={{0,7},{1,0},{2,1},{3,2},{4,3},{5,4},{6,5},{7,6},{8,15},{9,8},{10,9... | collective-permute-start | bytes 393224 | tf_op jit(solution)/shard_map/while/body/eval_jaxpr/ppermute | solution.py:56
  26.9 3.7 %collective-permute-start.5 = (f32[4,64,128]{2,1,0:T(8,128)S(1)}, f32[4,64,128]{2,1,0:T(8,128)S(1)}, u32[]{:S(2)}, u32[]{:S(2)}) collective-permute-start(f32[4,64,128]{2,1,0:T(8,128)S(1)} %collective-permute-done.3), channel_id=1, source_target_pairs={{0,7},{1,0},{2,1},{3,2},{4,3},{5,4},{6,5},{7,6},{8,15},{9,8},{10,9... | collective-permute-start | bytes 393224 | tf_op jit(solution)/shard_map/while/body/eval_jaxpr/ppermute | solution.py:56
  33.3 6.2 %collective-permute-done.6 = f32[4,64,128]{2,1,0:T(8,128)S(1)} collective-permute-done((f32[4,64,128]{2,1,0:T(8,128)S(1)}, f32[4,64,128]{2,1,0:T(8,128)S(1)}, u32[]{:S(2)}, u32[]{:S(2)}) %collective-permute-start.6) | collective-permute-done | bytes 131104 | tf_op jit(solution)/shard_map/while/body/eval_jaxpr/ppermute | solution.py:51
  39.5 8.9 %conditional.2 = (f32[4,64,128]{2,1,0:T(8,128)S(1)}) conditional(s32[]{:T(128)} %convert_element_type.11, () %tuple.137, (s32[]{:T(128)}, f32[4,64,128]{2,1,0:T(8,128)S(1)}, s32[]{:T(128)}, f32[4,64,128]{2,1,0:T(8,128)S(1)}, s32[]{:T(128)}, /*index=5*/s32[]{:T(128)}, f32[4,64,128]{2,1,0:T(8,128)S(1)}, s32[]{:T(128)}, ...), branch_computations={%region_1.1_spmd, %region_2.2_spmd.clone.clone} | conditional | flops 855672128 | bytes 14424849 | solution.py:63
  40.7 6.2 %convolution_bitcast_fusion = f32[4,64,128]{2,1,0:T(8,128)S(1)} fusion(f32[4,16,64,128]{3,2,1,0:T(8,128)S(1)} %bitcast.10, f32[4,128,16,128]{3,1,2,0:T(8,128)} %get-tuple-element.985), kind=kOutput, calls=%fused_computation.2 | convolution fusion | flops 805306368 | bytes 6422528 | tf_op jit(solution)/shard_map/while/body/eval_jaxpr/cond/branch_1_fun/jakb,jkwb->jwa/dot_general | solution.py:28
  53.2 3.5 %collective-permute-start.1 = (f32[4,64,128]{2,1,0:T(8,128)S(1)}, f32[4,64,128]{2,1,0:T(8,128)S(1)}, u32[]{:S(2)}, u32[]{:S(2)}) collective-permute-start(f32[4,64,128]{2,1,0:T(8,128)S(1)} %dynamic-slice_select_fusion.2), channel_id=1, source_target_pairs={{0,7},{1,0},{2,1},{3,2},{4,3},{5,4},{6,5},{7,6},{8,15},{9,8},{10,9... | collective-permute-start | bytes 393224 | tf_op jit(solution)/shard_map/while/body/eval_jaxpr/ppermute | solution.py:56
  59.5 3.6 %collective-permute-start.3 = (f32[4,64,128]{2,1,0:T(8,128)S(1)}, f32[4,64,128]{2,1,0:T(8,128)S(1)}, u32[]{:S(2)}, u32[]{:S(2)}) collective-permute-start(f32[4,64,128]{2,1,0:T(8,128)S(1)} %collective-permute-done.1), channel_id=1, source_target_pairs={{0,7},{1,0},{2,1},{3,2},{4,3},{5,4},{6,5},{7,6},{8,15},{9,8},{10,9... | collective-permute-start | bytes 393224 | tf_op jit(solution)/shard_map/while/body/eval_jaxpr/ppermute | solution.py:56
  65.8 3.6 %collective-permute-start.5 = (f32[4,64,128]{2,1,0:T(8,128)S(1)}, f32[4,64,128]{2,1,0:T(8,128)S(1)}, u32[]{:S(2)}, u32[]{:S(2)}) collective-permute-start(f32[4,64,128]{2,1,0:T(8,128)S(1)} %collective-permute-done.3), channel_id=1, source_target_pairs={{0,7},{1,0},{2,1},{3,2},{4,3},{5,4},{6,5},{7,6},{8,15},{9,8},{10,9... | collective-permute-start | bytes 393224 | tf_op jit(solution)/shard_map/while/body/eval_jaxpr/ppermute | solution.py:56
  72.0 6.2 %collective-permute-done.6 = f32[4,64,128]{2,1,0:T(8,128)S(1)} collective-permute-done((f32[4,64,128]{2,1,0:T(8,128)S(1)}, f32[4,64,128]{2,1,0:T(8,128)S(1)}, u32[]{:S(2)}, u32[]{:S(2)}) %collective-permute-start.6) | collective-permute-done | bytes 131104 | tf_op jit(solution)/shard_map/while/body/eval_jaxpr/ppermute | solution.py:51
  78.2 8.9 %conditional.2 = (f32[4,64,128]{2,1,0:T(8,128)S(1)}) conditional(s32[]{:T(128)} %convert_element_type.11, () %tuple.137, (s32[]{:T(128)}, f32[4,64,128]{2,1,0:T(8,128)S(1)}, s32[]{:T(128)}, f32[4,64,128]{2,1,0:T(8,128)S(1)}, s32[]{:T(128)}, /*index=5*/s32[]{:T(128)}, f32[4,64,128]{2,1,0:T(8,128)S(1)}, s32[]{:T(128)}, ...), branch_computations={%region_1.1_spmd, %region_2.2_spmd.clone.clone} | conditional | flops 855672128 | bytes 14424849 | solution.py:63
  79.4 6.2 %convolution_bitcast_fusion = f32[4,64,128]{2,1,0:T(8,128)S(1)} fusion(f32[4,16,64,128]{3,2,1,0:T(8,128)S(1)} %bitcast.10, f32[4,128,16,128]{3,1,2,0:T(8,128)} %get-tuple-element.985), kind=kOutput, calls=%fused_computation.2 | convolution fusion | flops 805306368 | bytes 6422528 | tf_op jit(solution)/shard_map/while/body/eval_jaxpr/cond/branch_1_fun/jakb,jkwb->jwa/dot_general | solution.py:28
  87.1 4.4 %collective-permute-start.7 = (f32[4,64,128]{2,1,0:T(8,128)S(1)}, f32[4,64,128]{2,1,0:T(8,128)S(1)}, u32[]{:S(2)}, u32[]{:S(2)}) collective-permute-start(f32[4,64,128]{2,1,0:T(8,128)S(1)} %get-tuple-element.1155), channel_id=1, source_target_pairs={{0,8},{1,9},{2,10},{3,11},{4,12},{5,13},{6,14},{7,15},{16,24},{17,... | collective-permute-start | bytes 393224 | tf_op jit(solution)/shard_map/while/body/eval_jaxpr/ppermute | solution.py:12
  101.3 3.5 %collective-permute-start.3 = (f32[4,64,128]{2,1,0:T(8,128)S(1)}, f32[4,64,128]{2,1,0:T(8,128)S(1)}, u32[]{:S(2)}, u32[]{:S(2)}) collective-permute-start(f32[4,64,128]{2,1,0:T(8,128)S(1)} %collective-permute-done.1), channel_id=1, source_target_pairs={{0,7},{1,0},{2,1},{3,2},{4,3},{5,4},{6,5},{7,6},{8,15},{9,8},{10,9... | collective-permute-start | bytes 393224 | tf_op jit(solution)/shard_map/while/body/eval_jaxpr/ppermute | solution.py:56
  107.6 3.5 %collective-permute-start.5 = (f32[4,64,128]{2,1,0:T(8,128)S(1)}, f32[4,64,128]{2,1,0:T(8,128)S(1)}, u32[]{:S(2)}, u32[]{:S(2)}) collective-permute-start(f32[4,64,128]{2,1,0:T(8,128)S(1)} %collective-permute-done.3), channel_id=1, source_target_pairs={{0,7},{1,0},{2,1},{3,2},{4,3},{5,4},{6,5},{7,6},{8,15},{9,8},{10,9... | collective-permute-start | bytes 393224 | tf_op jit(solution)/shard_map/while/body/eval_jaxpr/ppermute | solution.py:56
  113.8 6.2 %collective-permute-done.6 = f32[4,64,128]{2,1,0:T(8,128)S(1)} collective-permute-done((f32[4,64,128]{2,1,0:T(8,128)S(1)}, f32[4,64,128]{2,1,0:T(8,128)S(1)}, u32[]{:S(2)}, u32[]{:S(2)}) %collective-permute-start.6) | collective-permute-done | bytes 131104 | tf_op jit(solution)/shard_map/while/body/eval_jaxpr/ppermute | solution.py:51
  120.0 8.9 %conditional.2 = (f32[4,64,128]{2,1,0:T(8,128)S(1)}) conditional(s32[]{:T(128)} %convert_element_type.11, () %tuple.137, (s32[]{:T(128)}, f32[4,64,128]{2,1,0:T(8,128)S(1)}, s32[]{:T(128)}, f32[4,64,128]{2,1,0:T(8,128)S(1)}, s32[]{:T(128)}, /*index=5*/s32[]{:T(128)}, f32[4,64,128]{2,1,0:T(8,128)S(1)}, s32[]{:T(128)}, ...), branch_computations={%region_1.1_spmd, %region_2.2_spmd.clone.clone} | conditional | flops 855672128 | bytes 14424849 | solution.py:63
  121.2 6.2 %convolution_bitcast_fusion = f32[4,64,128]{2,1,0:T(8,128)S(1)} fusion(f32[4,16,64,128]{3,2,1,0:T(8,128)S(1)} %bitcast.10, f32[4,128,16,128]{3,1,2,0:T(8,128)} %get-tuple-element.985), kind=kOutput, calls=%fused_computation.2 | convolution fusion | flops 805306368 | bytes 6422528 | tf_op jit(solution)/shard_map/while/body/eval_jaxpr/cond/branch_1_fun/jakb,jkwb->jwa/dot_general | solution.py:28
  128.9 4.4 %collective-permute-start.7 = (f32[4,64,128]{2,1,0:T(8,128)S(1)}, f32[4,64,128]{2,1,0:T(8,128)S(1)}, u32[]{:S(2)}, u32[]{:S(2)}) collective-permute-start(f32[4,64,128]{2,1,0:T(8,128)S(1)} %get-tuple-element.1155), channel_id=1, source_target_pairs={{0,8},{1,9},{2,10},{3,11},{4,12},{5,13},{6,14},{7,15},{16,24},{17,... | collective-permute-start | bytes 393224 | tf_op jit(solution)/shard_map/while/body/eval_jaxpr/ppermute | solution.py:12
  143.0 3.5 %collective-permute-start.3 = (f32[4,64,128]{2,1,0:T(8,128)S(1)}, f32[4,64,128]{2,1,0:T(8,128)S(1)}, u32[]{:S(2)}, u32[]{:S(2)}) collective-permute-start(f32[4,64,128]{2,1,0:T(8,128)S(1)} %collective-permute-done.1), channel_id=1, source_target_pairs={{0,7},{1,0},{2,1},{3,2},{4,3},{5,4},{6,5},{7,6},{8,15},{9,8},{10,9... | collective-permute-start | bytes 393224 | tf_op jit(solution)/shard_map/while/body/eval_jaxpr/ppermute | solution.py:56
  149.3 3.5 %collective-permute-start.5 = (f32[4,64,128]{2,1,0:T(8,128)S(1)}, f32[4,64,128]{2,1,0:T(8,128)S(1)}, u32[]{:S(2)}, u32[]{:S(2)}) collective-permute-start(f32[4,64,128]{2,1,0:T(8,128)S(1)} %collective-permute-done.3), channel_id=1, source_target_pairs={{0,7},{1,0},{2,1},{3,2},{4,3},{5,4},{6,5},{7,6},{8,15},{9,8},{10,9... | collective-permute-start | bytes 393224 | tf_op jit(solution)/shard_map/while/body/eval_jaxpr/ppermute | solution.py:56
  155.5 6.2 %collective-permute-done.6 = f32[4,64,128]{2,1,0:T(8,128)S(1)} collective-permute-done((f32[4,64,128]{2,1,0:T(8,128)S(1)}, f32[4,64,128]{2,1,0:T(8,128)S(1)}, u32[]{:S(2)}, u32[]{:S(2)}) %collective-permute-start.6) | collective-permute-done | bytes 131104 | tf_op jit(solution)/shard_map/while/body/eval_jaxpr/ppermute | solution.py:51
  161.7 8.9 %conditional.2 = (f32[4,64,128]{2,1,0:T(8,128)S(1)}) conditional(s32[]{:T(128)} %convert_element_type.11, () %tuple.137, (s32[]{:T(128)}, f32[4,64,128]{2,1,0:T(8,128)S(1)}, s32[]{:T(128)}, f32[4,64,128]{2,1,0:T(8,128)S(1)}, s32[]{:T(128)}, /*index=5*/s32[]{:T(128)}, f32[4,64,128]{2,1,0:T(8,128)S(1)}, s32[]{:T(128)}, ...), branch_computations={%region_1.1_spmd, %region_2.2_spmd.clone.clone} | conditional | flops 855672128 | bytes 14424849 | solution.py:63
  162.9 6.2 %convolution_bitcast_fusion = f32[4,64,128]{2,1,0:T(8,128)S(1)} fusion(f32[4,16,64,128]{3,2,1,0:T(8,128)S(1)} %bitcast.10, f32[4,128,16,128]{3,1,2,0:T(8,128)} %get-tuple-element.985), kind=kOutput, calls=%fused_computation.2 | convolution fusion | flops 805306368 | bytes 6422528 | tf_op jit(solution)/shard_map/while/body/eval_jaxpr/cond/branch_1_fun/jakb,jkwb->jwa/dot_general | solution.py:28
  170.6 4.4 %collective-permute-start.7 = (f32[4,64,128]{2,1,0:T(8,128)S(1)}, f32[4,64,128]{2,1,0:T(8,128)S(1)}, u32[]{:S(2)}, u32[]{:S(2)}) collective-permute-start(f32[4,64,128]{2,1,0:T(8,128)S(1)} %get-tuple-element.1155), channel_id=1, source_target_pairs={{0,8},{1,9},{2,10},{3,11},{4,12},{5,13},{6,14},{7,15},{16,24},{17,... | collective-permute-start | bytes 393224 | tf_op jit(solution)/shard_map/while/body/eval_jaxpr/ppermute | solution.py:12
  184.8 3.5 %collective-permute-start.3 = (f32[4,64,128]{2,1,0:T(8,128)S(1)}, f32[4,64,128]{2,1,0:T(8,128)S(1)}, u32[]{:S(2)}, u32[]{:S(2)}) collective-permute-start(f32[4,64,128]{2,1,0:T(8,128)S(1)} %collective-permute-done.1), channel_id=1, source_target_pairs={{0,7},{1,0},{2,1},{3,2},{4,3},{5,4},{6,5},{7,6},{8,15},{9,8},{10,9... | collective-permute-start | bytes 393224 | tf_op jit(solution)/shard_map/while/body/eval_jaxpr/ppermute | solution.py:56
  191.1 3.5 %collective-permute-start.5 = (f32[4,64,128]{2,1,0:T(8,128)S(1)}, f32[4,64,128]{2,1,0:T(8,128)S(1)}, u32[]{:S(2)}, u32[]{:S(2)}) collective-permute-start(f32[4,64,128]{2,1,0:T(8,128)S(1)} %collective-permute-done.3), channel_id=1, source_target_pairs={{0,7},{1,0},{2,1},{3,2},{4,3},{5,4},{6,5},{7,6},{8,15},{9,8},{10,9... | collective-permute-start | bytes 393224 | tf_op jit(solution)/shard_map/while/body/eval_jaxpr/ppermute | solution.py:56
  197.3 6.2 %collective-permute-done.6 = f32[4,64,128]{2,1,0:T(8,128)S(1)} collective-permute-done((f32[4,64,128]{2,1,0:T(8,128)S(1)}, f32[4,64,128]{2,1,0:T(8,128)S(1)}, u32[]{:S(2)}, u32[]{:S(2)}) %collective-permute-start.6) | collective-permute-done | bytes 131104 | tf_op jit(solution)/shard_map/while/body/eval_jaxpr/ppermute | solution.py:51
  203.5 13.3 %collective-permute-start.7 = (f32[4,64,128]{2,1,0:T(8,128)S(1)}, f32[4,64,128]{2,1,0:T(8,128)S(1)}, u32[]{:S(2)}, u32[]{:S(2)}) collective-permute-start(f32[4,64,128]{2,1,0:T(8,128)S(1)} %get-tuple-element.1155), channel_id=1, source_target_pairs={{0,8},{1,9},{2,10},{3,11},{4,12},{5,13},{6,14},{7,15},{16,24},{17,... | collective-permute-start | bytes 393224 | tf_op jit(solution)/shard_map/while/body/eval_jaxpr/ppermute | solution.py:12
  (133 shorter events, 82.1 us)
Async XLA Ops:
  12.6 7.3 %collective-permute-start = (f32[4,64,128]{2,1,0:T(8,128)S(1)}, f32[4,64,128]{2,1,0:T(8,128)S(1)}, u32[]{:S(2)}, u32[]{:S(2)}) collective-permute-start(f32[4,64,128]{2,1,0:T(8,128)S(1)} %dynamic-slice_select_fusion.2), channel_id=1, source_target_pairs={{0,1},{1,2},{2,3},{3,4},{4,5},{5,6},{6,7},{7,0},{8,9},{9,10},{10,1... | collective-permute-start | bytes 393224 | tf_op jit(solution)/shard_map/while/body/eval_jaxpr/ppermute | solution.py:51
  13.2 6.8 %collective-permute-start.1 = (f32[4,64,128]{2,1,0:T(8,128)S(1)}, f32[4,64,128]{2,1,0:T(8,128)S(1)}, u32[]{:S(2)}, u32[]{:S(2)}) collective-permute-start(f32[4,64,128]{2,1,0:T(8,128)S(1)} %dynamic-slice_select_fusion.2), channel_id=1, source_target_pairs={{0,7},{1,0},{2,1},{3,2},{4,3},{5,4},{6,5},{7,6},{8,15},{9,8},{10,9... | collective-permute-start | bytes 393224 | tf_op jit(solution)/shard_map/while/body/eval_jaxpr/ppermute | solution.py:56
  19.9 6.9 %collective-permute-start.2 = (f32[4,64,128]{2,1,0:T(8,128)S(1)}, f32[4,64,128]{2,1,0:T(8,128)S(1)}, u32[]{:S(2)}, u32[]{:S(2)}) collective-permute-start(f32[4,64,128]{2,1,0:T(8,128)S(1)} %collective-permute-done), channel_id=1, source_target_pairs={{0,1},{1,2},{2,3},{3,4},{4,5},{5,6},{6,7},{7,0},{8,9},{9,10},{10,1... | collective-permute-start | bytes 393224 | tf_op jit(solution)/shard_map/while/body/eval_jaxpr/ppermute | solution.py:51
  19.9 7.0 %collective-permute-start.3 = (f32[4,64,128]{2,1,0:T(8,128)S(1)}, f32[4,64,128]{2,1,0:T(8,128)S(1)}, u32[]{:S(2)}, u32[]{:S(2)}) collective-permute-start(f32[4,64,128]{2,1,0:T(8,128)S(1)} %collective-permute-done.1), channel_id=1, source_target_pairs={{0,7},{1,0},{2,1},{3,2},{4,3},{5,4},{6,5},{7,6},{8,15},{9,8},{10,9... | collective-permute-start | bytes 393224 | tf_op jit(solution)/shard_map/while/body/eval_jaxpr/ppermute | solution.py:56
  26.8 6.5 %collective-permute-start.4 = (f32[4,64,128]{2,1,0:T(8,128)S(1)}, f32[4,64,128]{2,1,0:T(8,128)S(1)}, u32[]{:S(2)}, u32[]{:S(2)}) collective-permute-start(f32[4,64,128]{2,1,0:T(8,128)S(1)} %collective-permute-done.2), channel_id=1, source_target_pairs={{0,1},{1,2},{2,3},{3,4},{4,5},{5,6},{6,7},{7,0},{8,9},{9,10},{10,1... | collective-permute-start | bytes 393224 | tf_op jit(solution)/shard_map/while/body/eval_jaxpr/ppermute | solution.py:51
  26.9 6.4 %collective-permute-start.5 = (f32[4,64,128]{2,1,0:T(8,128)S(1)}, f32[4,64,128]{2,1,0:T(8,128)S(1)}, u32[]{:S(2)}, u32[]{:S(2)}) collective-permute-start(f32[4,64,128]{2,1,0:T(8,128)S(1)} %collective-permute-done.3), channel_id=1, source_target_pairs={{0,7},{1,0},{2,1},{3,2},{4,3},{5,4},{6,5},{7,6},{8,15},{9,8},{10,9... | collective-permute-start | bytes 393224 | tf_op jit(solution)/shard_map/while/body/eval_jaxpr/ppermute | solution.py:56
  33.3 6.2 %collective-permute-start.6 = (f32[4,64,128]{2,1,0:T(8,128)S(1)}, f32[4,64,128]{2,1,0:T(8,128)S(1)}, u32[]{:S(2)}, u32[]{:S(2)}) collective-permute-start(f32[4,64,128]{2,1,0:T(8,128)S(1)} %collective-permute-done.4), channel_id=1, source_target_pairs={{0,1},{1,2},{2,3},{3,4},{4,5},{5,6},{6,7},{7,0},{8,9},{9,10},{10,1... | collective-permute-start | bytes 393224 | tf_op jit(solution)/shard_map/while/body/eval_jaxpr/ppermute | solution.py:51
  53.2 6.3 %collective-permute-start = (f32[4,64,128]{2,1,0:T(8,128)S(1)}, f32[4,64,128]{2,1,0:T(8,128)S(1)}, u32[]{:S(2)}, u32[]{:S(2)}) collective-permute-start(f32[4,64,128]{2,1,0:T(8,128)S(1)} %dynamic-slice_select_fusion.2), channel_id=1, source_target_pairs={{0,1},{1,2},{2,3},{3,4},{4,5},{5,6},{6,7},{7,0},{8,9},{9,10},{10,1... | collective-permute-start | bytes 393224 | tf_op jit(solution)/shard_map/while/body/eval_jaxpr/ppermute | solution.py:51
  53.2 6.3 %collective-permute-start.1 = (f32[4,64,128]{2,1,0:T(8,128)S(1)}, f32[4,64,128]{2,1,0:T(8,128)S(1)}, u32[]{:S(2)}, u32[]{:S(2)}) collective-permute-start(f32[4,64,128]{2,1,0:T(8,128)S(1)} %dynamic-slice_select_fusion.2), channel_id=1, source_target_pairs={{0,7},{1,0},{2,1},{3,2},{4,3},{5,4},{6,5},{7,6},{8,15},{9,8},{10,9... | collective-permute-start | bytes 393224 | tf_op jit(solution)/shard_map/while/body/eval_jaxpr/ppermute | solution.py:56
  59.5 6.3 %collective-permute-start.2 = (f32[4,64,128]{2,1,0:T(8,128)S(1)}, f32[4,64,128]{2,1,0:T(8,128)S(1)}, u32[]{:S(2)}, u32[]{:S(2)}) collective-permute-start(f32[4,64,128]{2,1,0:T(8,128)S(1)} %collective-permute-done), channel_id=1, source_target_pairs={{0,1},{1,2},{2,3},{3,4},{4,5},{5,6},{6,7},{7,0},{8,9},{9,10},{10,1... | collective-permute-start | bytes 393224 | tf_op jit(solution)/shard_map/while/body/eval_jaxpr/ppermute | solution.py:51
  59.5 6.3 %collective-permute-start.3 = (f32[4,64,128]{2,1,0:T(8,128)S(1)}, f32[4,64,128]{2,1,0:T(8,128)S(1)}, u32[]{:S(2)}, u32[]{:S(2)}) collective-permute-start(f32[4,64,128]{2,1,0:T(8,128)S(1)} %collective-permute-done.1), channel_id=1, source_target_pairs={{0,7},{1,0},{2,1},{3,2},{4,3},{5,4},{6,5},{7,6},{8,15},{9,8},{10,9... | collective-permute-start | bytes 393224 | tf_op jit(solution)/shard_map/while/body/eval_jaxpr/ppermute | solution.py:56
  87.1 6.9 %collective-permute-start.7 = (f32[4,64,128]{2,1,0:T(8,128)S(1)}, f32[4,64,128]{2,1,0:T(8,128)S(1)}, u32[]{:S(2)}, u32[]{:S(2)}) collective-permute-start(f32[4,64,128]{2,1,0:T(8,128)S(1)} %get-tuple-element.1155), channel_id=1, source_target_pairs={{0,8},{1,9},{2,10},{3,11},{4,12},{5,13},{6,14},{7,15},{16,24},{17,... | collective-permute-start | bytes 393224 | tf_op jit(solution)/shard_map/while/body/eval_jaxpr/ppermute | solution.py:12
  94.9 6.3 %collective-permute-start = (f32[4,64,128]{2,1,0:T(8,128)S(1)}, f32[4,64,128]{2,1,0:T(8,128)S(1)}, u32[]{:S(2)}, u32[]{:S(2)}) collective-permute-start(f32[4,64,128]{2,1,0:T(8,128)S(1)} %dynamic-slice_select_fusion.2), channel_id=1, source_target_pairs={{0,1},{1,2},{2,3},{3,4},{4,5},{5,6},{6,7},{7,0},{8,9},{9,10},{10,1... | collective-permute-start | bytes 393224 | tf_op jit(solution)/shard_map/while/body/eval_jaxpr/ppermute | solution.py:51
  95.0 6.3 %collective-permute-start.1 = (f32[4,64,128]{2,1,0:T(8,128)S(1)}, f32[4,64,128]{2,1,0:T(8,128)S(1)}, u32[]{:S(2)}, u32[]{:S(2)}) collective-permute-start(f32[4,64,128]{2,1,0:T(8,128)S(1)} %dynamic-slice_select_fusion.2), channel_id=1, source_target_pairs={{0,7},{1,0},{2,1},{3,2},{4,3},{5,4},{6,5},{7,6},{8,15},{9,8},{10,9... | collective-permute-start | bytes 393224 | tf_op jit(solution)/shard_map/while/body/eval_jaxpr/ppermute | solution.py:56
  101.3 6.3 %collective-permute-start.2 = (f32[4,64,128]{2,1,0:T(8,128)S(1)}, f32[4,64,128]{2,1,0:T(8,128)S(1)}, u32[]{:S(2)}, u32[]{:S(2)}) collective-permute-start(f32[4,64,128]{2,1,0:T(8,128)S(1)} %collective-permute-done), channel_id=1, source_target_pairs={{0,1},{1,2},{2,3},{3,4},{4,5},{5,6},{6,7},{7,0},{8,9},{9,10},{10,1... | collective-permute-start | bytes 393224 | tf_op jit(solution)/shard_map/while/body/eval_jaxpr/ppermute | solution.py:51
  101.3 6.3 %collective-permute-start.3 = (f32[4,64,128]{2,1,0:T(8,128)S(1)}, f32[4,64,128]{2,1,0:T(8,128)S(1)}, u32[]{:S(2)}, u32[]{:S(2)}) collective-permute-start(f32[4,64,128]{2,1,0:T(8,128)S(1)} %collective-permute-done.1), channel_id=1, source_target_pairs={{0,7},{1,0},{2,1},{3,2},{4,3},{5,4},{6,5},{7,6},{8,15},{9,8},{10,9... | collective-permute-start | bytes 393224 | tf_op jit(solution)/shard_map/while/body/eval_jaxpr/ppermute | solution.py:56
  107.6 6.2 %collective-permute-start.4 = (f32[4,64,128]{2,1,0:T(8,128)S(1)}, f32[4,64,128]{2,1,0:T(8,128)S(1)}, u32[]{:S(2)}, u32[]{:S(2)}) collective-permute-start(f32[4,64,128]{2,1,0:T(8,128)S(1)} %collective-permute-done.2), channel_id=1, source_target_pairs={{0,1},{1,2},{2,3},{3,4},{4,5},{5,6},{6,7},{7,0},{8,9},{9,10},{10,1... | collective-permute-start | bytes 393224 | tf_op jit(solution)/shard_map/while/body/eval_jaxpr/ppermute | solution.py:51
  107.6 6.2 %collective-permute-start.5 = (f32[4,64,128]{2,1,0:T(8,128)S(1)}, f32[4,64,128]{2,1,0:T(8,128)S(1)}, u32[]{:S(2)}, u32[]{:S(2)}) collective-permute-start(f32[4,64,128]{2,1,0:T(8,128)S(1)} %collective-permute-done.3), channel_id=1, source_target_pairs={{0,7},{1,0},{2,1},{3,2},{4,3},{5,4},{6,5},{7,6},{8,15},{9,8},{10,9... | collective-permute-start | bytes 393224 | tf_op jit(solution)/shard_map/while/body/eval_jaxpr/ppermute | solution.py:56
  113.8 6.2 %collective-permute-start.6 = (f32[4,64,128]{2,1,0:T(8,128)S(1)}, f32[4,64,128]{2,1,0:T(8,128)S(1)}, u32[]{:S(2)}, u32[]{:S(2)}) collective-permute-start(f32[4,64,128]{2,1,0:T(8,128)S(1)} %collective-permute-done.4), channel_id=1, source_target_pairs={{0,1},{1,2},{2,3},{3,4},{4,5},{5,6},{6,7},{7,0},{8,9},{9,10},{10,1... | collective-permute-start | bytes 393224 | tf_op jit(solution)/shard_map/while/body/eval_jaxpr/ppermute | solution.py:51
  128.9 6.9 %collective-permute-start.7 = (f32[4,64,128]{2,1,0:T(8,128)S(1)}, f32[4,64,128]{2,1,0:T(8,128)S(1)}, u32[]{:S(2)}, u32[]{:S(2)}) collective-permute-start(f32[4,64,128]{2,1,0:T(8,128)S(1)} %get-tuple-element.1155), channel_id=1, source_target_pairs={{0,8},{1,9},{2,10},{3,11},{4,12},{5,13},{6,14},{7,15},{16,24},{17,... | collective-permute-start | bytes 393224 | tf_op jit(solution)/shard_map/while/body/eval_jaxpr/ppermute | solution.py:12
  136.7 6.3 %collective-permute-start = (f32[4,64,128]{2,1,0:T(8,128)S(1)}, f32[4,64,128]{2,1,0:T(8,128)S(1)}, u32[]{:S(2)}, u32[]{:S(2)}) collective-permute-start(f32[4,64,128]{2,1,0:T(8,128)S(1)} %dynamic-slice_select_fusion.2), channel_id=1, source_target_pairs={{0,1},{1,2},{2,3},{3,4},{4,5},{5,6},{6,7},{7,0},{8,9},{9,10},{10,1... | collective-permute-start | bytes 393224 | tf_op jit(solution)/shard_map/while/body/eval_jaxpr/ppermute | solution.py:51
  136.7 6.3 %collective-permute-start.1 = (f32[4,64,128]{2,1,0:T(8,128)S(1)}, f32[4,64,128]{2,1,0:T(8,128)S(1)}, u32[]{:S(2)}, u32[]{:S(2)}) collective-permute-start(f32[4,64,128]{2,1,0:T(8,128)S(1)} %dynamic-slice_select_fusion.2), channel_id=1, source_target_pairs={{0,7},{1,0},{2,1},{3,2},{4,3},{5,4},{6,5},{7,6},{8,15},{9,8},{10,9... | collective-permute-start | bytes 393224 | tf_op jit(solution)/shard_map/while/body/eval_jaxpr/ppermute | solution.py:56
  143.0 6.3 %collective-permute-start.2 = (f32[4,64,128]{2,1,0:T(8,128)S(1)}, f32[4,64,128]{2,1,0:T(8,128)S(1)}, u32[]{:S(2)}, u32[]{:S(2)}) collective-permute-start(f32[4,64,128]{2,1,0:T(8,128)S(1)} %collective-permute-done), channel_id=1, source_target_pairs={{0,1},{1,2},{2,3},{3,4},{4,5},{5,6},{6,7},{7,0},{8,9},{9,10},{10,1... | collective-permute-start | bytes 393224 | tf_op jit(solution)/shard_map/while/body/eval_jaxpr/ppermute | solution.py:51
  143.0 6.3 %collective-permute-start.3 = (f32[4,64,128]{2,1,0:T(8,128)S(1)}, f32[4,64,128]{2,1,0:T(8,128)S(1)}, u32[]{:S(2)}, u32[]{:S(2)}) collective-permute-start(f32[4,64,128]{2,1,0:T(8,128)S(1)} %collective-permute-done.1), channel_id=1, source_target_pairs={{0,7},{1,0},{2,1},{3,2},{4,3},{5,4},{6,5},{7,6},{8,15},{9,8},{10,9... | collective-permute-start | bytes 393224 | tf_op jit(solution)/shard_map/while/body/eval_jaxpr/ppermute | solution.py:56
  149.3 6.2 %collective-permute-start.4 = (f32[4,64,128]{2,1,0:T(8,128)S(1)}, f32[4,64,128]{2,1,0:T(8,128)S(1)}, u32[]{:S(2)}, u32[]{:S(2)}) collective-permute-start(f32[4,64,128]{2,1,0:T(8,128)S(1)} %collective-permute-done.2), channel_id=1, source_target_pairs={{0,1},{1,2},{2,3},{3,4},{4,5},{5,6},{6,7},{7,0},{8,9},{9,10},{10,1... | collective-permute-start | bytes 393224 | tf_op jit(solution)/shard_map/while/body/eval_jaxpr/ppermute | solution.py:51
  149.3 6.2 %collective-permute-start.5 = (f32[4,64,128]{2,1,0:T(8,128)S(1)}, f32[4,64,128]{2,1,0:T(8,128)S(1)}, u32[]{:S(2)}, u32[]{:S(2)}) collective-permute-start(f32[4,64,128]{2,1,0:T(8,128)S(1)} %collective-permute-done.3), channel_id=1, source_target_pairs={{0,7},{1,0},{2,1},{3,2},{4,3},{5,4},{6,5},{7,6},{8,15},{9,8},{10,9... | collective-permute-start | bytes 393224 | tf_op jit(solution)/shard_map/while/body/eval_jaxpr/ppermute | solution.py:56
  170.6 6.9 %collective-permute-start.7 = (f32[4,64,128]{2,1,0:T(8,128)S(1)}, f32[4,64,128]{2,1,0:T(8,128)S(1)}, u32[]{:S(2)}, u32[]{:S(2)}) collective-permute-start(f32[4,64,128]{2,1,0:T(8,128)S(1)} %get-tuple-element.1155), channel_id=1, source_target_pairs={{0,8},{1,9},{2,10},{3,11},{4,12},{5,13},{6,14},{7,15},{16,24},{17,... | collective-permute-start | bytes 393224 | tf_op jit(solution)/shard_map/while/body/eval_jaxpr/ppermute | solution.py:12
  178.4 6.3 %collective-permute-start = (f32[4,64,128]{2,1,0:T(8,128)S(1)}, f32[4,64,128]{2,1,0:T(8,128)S(1)}, u32[]{:S(2)}, u32[]{:S(2)}) collective-permute-start(f32[4,64,128]{2,1,0:T(8,128)S(1)} %dynamic-slice_select_fusion.2), channel_id=1, source_target_pairs={{0,1},{1,2},{2,3},{3,4},{4,5},{5,6},{6,7},{7,0},{8,9},{9,10},{10,1... | collective-permute-start | bytes 393224 | tf_op jit(solution)/shard_map/while/body/eval_jaxpr/ppermute | solution.py:51
  178.5 6.3 %collective-permute-start.1 = (f32[4,64,128]{2,1,0:T(8,128)S(1)}, f32[4,64,128]{2,1,0:T(8,128)S(1)}, u32[]{:S(2)}, u32[]{:S(2)}) collective-permute-start(f32[4,64,128]{2,1,0:T(8,128)S(1)} %dynamic-slice_select_fusion.2), channel_id=1, source_target_pairs={{0,7},{1,0},{2,1},{3,2},{4,3},{5,4},{6,5},{7,6},{8,15},{9,8},{10,9... | collective-permute-start | bytes 393224 | tf_op jit(solution)/shard_map/while/body/eval_jaxpr/ppermute | solution.py:56
  184.8 6.3 %collective-permute-start.2 = (f32[4,64,128]{2,1,0:T(8,128)S(1)}, f32[4,64,128]{2,1,0:T(8,128)S(1)}, u32[]{:S(2)}, u32[]{:S(2)}) collective-permute-start(f32[4,64,128]{2,1,0:T(8,128)S(1)} %collective-permute-done), channel_id=1, source_target_pairs={{0,1},{1,2},{2,3},{3,4},{4,5},{5,6},{6,7},{7,0},{8,9},{9,10},{10,1... | collective-permute-start | bytes 393224 | tf_op jit(solution)/shard_map/while/body/eval_jaxpr/ppermute | solution.py:51
  184.8 6.3 %collective-permute-start.3 = (f32[4,64,128]{2,1,0:T(8,128)S(1)}, f32[4,64,128]{2,1,0:T(8,128)S(1)}, u32[]{:S(2)}, u32[]{:S(2)}) collective-permute-start(f32[4,64,128]{2,1,0:T(8,128)S(1)} %collective-permute-done.1), channel_id=1, source_target_pairs={{0,7},{1,0},{2,1},{3,2},{4,3},{5,4},{6,5},{7,6},{8,15},{9,8},{10,9... | collective-permute-start | bytes 393224 | tf_op jit(solution)/shard_map/while/body/eval_jaxpr/ppermute | solution.py:56
  203.5 15.8 %collective-permute-start.7 = (f32[4,64,128]{2,1,0:T(8,128)S(1)}, f32[4,64,128]{2,1,0:T(8,128)S(1)}, u32[]{:S(2)}, u32[]{:S(2)}) collective-permute-start(f32[4,64,128]{2,1,0:T(8,128)S(1)} %get-tuple-element.1155), channel_id=1, source_target_pairs={{0,8},{1,9},{2,10},{3,11},{4,12},{5,13},{6,14},{7,15},{16,24},{17,... | collective-permute-start | bytes 393224 | tf_op jit(solution)/shard_map/while/body/eval_jaxpr/ppermute | solution.py:12
  (10 other events, 59.7 us)
